TPU v7x, 256 devices: a whole 4x4x8 slice. The times are simulated.
256 devices in a mesh: row: 8 (over x_hi, y), col: 32 (over z, x_lo, core).
Axes of the slice: x: 4 (x_hi: 2, x_lo: 2; x = x_hi * 2 + x_lo), y: 4, z: 8, core: 2. Of those that a mesh axis runs over, the one named last changes fastest.
Arguments:
- region_inverse: float32 [4096, 4096], P('row', 'col'), may hold values from -6 to 6
- factor_cols: float32 [3, 4096, 512], P(None, 'row'), may hold values from -0.09375 to 0.09375
- parent_factor: float32 [2, 512, 512], P(None, 'col'), may hold values from -0.25 to 0.25
- diag_inverse: float32 [3, 512, 512], P(None, 'col'), may hold values from -6 to 6
- listed: int32 [3, 8], replicated, may hold values from 0 to 1, as said below
Outputs:
- col_blocks: float32 [3, 4096, 512], P(None, ('row', 'col'))
- diag_blocks: float32 [3, 512, 512], P(None, 'col')
- parent_rows: float32 [2, 512, 512], P(None, 'col')
Inputs may be any that keep to these rules, and one draw needn't show every extreme that they name: listed[0] has exactly 6 ones; listed[1] and listed[2] have exactly 4 ones each, all at blocks that listed[0] also lists.
All inputs are finite; a program needn't handle non-finite values.
Results may differ from a plain program's by a relative error of at most 0.0001.
Values sent between devices are 32-bit elements; how exact they have to be, the bound alone decides.
A program may use at most 64 MiB of HBM per device.

v0:
```python
import jax
import jax.numpy as jnp
from jax import lax
from jax.sharding import PartitionSpec as P


def broadcast(value, axis, source):
    kept = jnp.where(lax.axis_index(axis) == source, value, 0).astype(value.dtype)
    return lax.psum(kept, axis)


def matmul_plain(left, right):
    return jnp.dot(left, right, precision=lax.Precision.HIGHEST, preferred_element_type=jnp.float32)


def matmul_left(left, right):
    return lax.dot_general(
        left,
        right,
        (((0,), (0,)), ((), ())),
        precision=lax.Precision.HIGHEST,
        preferred_element_type=jnp.float32,
    )


def row_weights(listed_row, first_row, count, width):
    global_rows = first_row + lax.iota(jnp.int32, count)
    block_ids = global_rows // width
    table = lax.iota(jnp.int32, listed_row.shape[0])
    hits = (block_ids[:, None] == table[None, :]).astype(jnp.float32) * listed_row.astype(
        jnp.float32
    )[None, :]
    return jnp.sum(hits, axis=1)


def total_sums(values):
    return lax.psum(tuple(values), ("row", "col"))


def shards(region_inverse, factor_cols, parent_factor, diag_inverse, listed):
    row_count = lax.axis_size("row")
    col_count = lax.axis_size("col")
    row_place = lax.axis_index("row")
    col_place = lax.axis_index("col")
    rows_here, cols_here = region_inverse.shape
    width = factor_cols.shape[2]
    group = rows_here // col_count
    ratio = col_count // row_count
    diag_width = width // col_count
    diag_start = col_place * diag_width
    full_diag, full_parent = (
        lax.all_gather(diag_inverse, "col", axis=1, tiled=True),
        lax.all_gather(parent_factor, "col", axis=1, tiled=True),
    )
    masks = [
        row_weights(listed[member], row_place * rows_here, rows_here, width) for member in range(3)
    ]
    factors = [factor_cols[member] * masks[member][:, None] for member in range(3)]
    group_masks = [
        lax.dynamic_slice_in_dim(masks[member], col_place * group, group, 0) for member in range(3)
    ]
    pieces = [
        lax.dynamic_slice_in_dim(factors[member], col_place * group, group, 0)
        for member in range(3)
    ]

    def column_pass(members, extra_rows):
        slices = [
            lax.dynamic_slice_in_dim(factors[member], col_place % ratio * cols_here, cols_here, 0)
            for member in members
        ]
        stacked = jnp.stack(slices, axis=1)
        received = broadcast(stacked, "row", col_place // ratio)
        right_side = received.reshape(cols_here, len(members) * width)
        summed = lax.psum_scatter(
            matmul_plain(region_inverse, right_side), "col", scatter_dimension=0, tiled=True
        )
        outputs = []
        terms = []
        for place, member in enumerate(members):
            partial_sum = summed
            if extra_rows[place] is not None:
                partial_sum = partial_sum + extra_rows[place]
            column = -partial_sum * group_masks[member][:, None]
            outputs.append(column)
            terms.append(-matmul_left(pieces[member], column))
        return (outputs, terms)

    parent_out, parent_terms = column_pass([0], [None])
    parent_col = parent_out[0]
    parent_totals = total_sums(parent_terms)
    parent_diag = full_diag[0] + parent_totals[0]
    parent_slice = lax.dynamic_slice_in_dim(parent_diag, diag_start, diag_width, 0)
    links = [full_parent[0], full_parent[1]]
    extra_rows = [matmul_plain(parent_col, links[place]) for place in range(2)]
    extra_sums = [matmul_left(parent_col, pieces[place + 1]) for place in range(2)]
    child_cols = []
    diag_list = [parent_slice]
    upper_list = []
    for place in range(2):
        outputs, terms = column_pass([place + 1], [extra_rows[place]])
        child_cols.append(outputs[0])
        link_terms = [extra_sums[place]]
        places = [place]
        count = len(places)
        diags = []
        uppers = []
        totals = total_sums(list(terms) + list(link_terms))
        for k, finish_place in enumerate(places):
            link_cols = lax.dynamic_slice_in_dim(links[finish_place], diag_start, diag_width, 1)
            upper_total = totals[count + k]
            upper_slice = -(
                lax.dynamic_slice_in_dim(upper_total, diag_start, diag_width, 0)
                + matmul_plain(parent_slice, links[finish_place])
            )
            weighted_diag = matmul_left(link_cols, parent_diag)
            link_upper = -(
                matmul_left(link_cols, upper_total)
                + matmul_plain(weighted_diag, links[finish_place])
            )
            diag_rows = lax.dynamic_slice_in_dim(
                full_diag[finish_place + 1], diag_start, diag_width, 0
            )
            total_rows = lax.dynamic_slice_in_dim(totals[k], diag_start, diag_width, 0)
            diags.append(diag_rows + total_rows - link_upper)
            uppers.append(upper_slice)
        diags, uppers = (diags, uppers)
        diag_list = diag_list + diags
        upper_list = upper_list + uppers
    col_blocks = jnp.stack([parent_col] + child_cols)
    diag_blocks = jnp.stack(diag_list)
    parent_rows = jnp.stack(upper_list)
    return (col_blocks, diag_blocks, parent_rows)


def solution(mesh):
    in_specs = (
        P("row", "col"),
        P(None, "row", None),
        P(None, "col", None),
        P(None, "col", None),
        P(),
    )
    out_specs = (P(None, ("row", "col"), None), P(None, "col", None), P(None, "col", None))
    return jax.shard_map(shards, mesh=mesh, in_specs=in_specs, out_specs=out_specs, check_vma=False)
```

profile of v0, /device:TPU:8, one launch (start us, length us, event | category | flops | bytes accessed | tf_op | source)
XLA Modules:
  0.0 894.7 jit_solution(15378608520947166456)
XLA Ops:
  7.2 0.0 copy-start
  7.2 0.0 all-reduce.7.cloned.1.call-start
  7.3 0.8 convert_bitcast_fusion.2
  8.1 0.1 select_reduce_fusion.1
  8.2 2.1 bitcast_multiply_fusion.1
  10.3 0.0 copy-start.4
  10.3 0.8 dynamic-slice_select_fusion.2
  11.2 0.2 copy-done.4
  11.4 0.9 dynamic-slice_select_fusion
  12.3 0.0 all-reduce.7.cloned.1.call-update
  12.3 0.0 reduce-scatter.10.cloned.1.call-start
  12.3 91.4 %all-reduce.7.cloned.1.call-done = (f32[128,512]{1,0:T(8,128)}, f32[128,512]{1,0:T(8,128)}, f32[128,512]{1,0:T(8,128)}) async-done(((f32[128,512]{1,0:T(8,128)}, f32[128,512]{1,0:T(8,128)}, f32[128,512]{1,0:T(8,128)}), (f32[128,512]{1,0:T(8,128)}, f32[128,512]{1,0:T(8,128)}, f32[128,512]{1,0:T(8,128)})) %all-reduce.7.cloned.1.call-update) | async-done | bytes 786448 | tf_op jit(solution)/shard_map/psum | solution.py:9
  103.8 2.0 convolution_bitcast_fusion.2
  105.8 1.4 copy.17
  107.2 0.0 reduce-scatter.10.cloned.1.call-update
  107.2 0.0 reduce-scatter.12.cloned.1.call-start
  107.3 1.0 convolution_bitcast_fusion.1
  108.3 1.3 copy.19
  109.6 0.0 reduce-scatter.12.cloned.1.call-update
  109.7 0.0 all-gather.3.cloned.1.call-start
  109.7 0.5 all-gather.3.cloned.1.call-update
  110.2 0.0 reduce-scatter.14.cloned.1.call-start
  110.3 0.0 copy-done.8
  110.3 1.0 convolution_bitcast_fusion
  111.3 1.3 copy.21
  112.7 0.0 reduce-scatter.14.cloned.1.call-update
  112.7 0.0 all-gather.5.cloned.1.call-start
  112.8 0.5 all-gather.5.cloned.1.call-update
  113.3 0.2 all-reduce.5.cloned.1.call-start
  113.5 0.1 dynamic_slice.63
  113.6 0.1 dynamic_slice.65
  113.7 0.1 dynamic_slice.67
  113.7 113.7 %reduce-scatter.10.cloned.1.call-done = f32[16,512]{1,0:T(8,128)} async-done(((f32[512,512]{1,0:T(8,128)}), f32[16,512]{1,0:T(8,128)}) %reduce-scatter.10.cloned.1.call-update) | async-done | bytes 32784
  227.4 0.9 copy.18
  228.3 2.9 convolution_negate_fusion.2
  231.2 2.0 fusion.33
  233.2 2.7 fusion.34
  235.9 110.6 %reduce-scatter.12.cloned.1.call-done = f32[16,512]{1,0:T(8,128)} async-done(((f32[512,512]{1,0:T(8,128)}), f32[16,512]{1,0:T(8,128)}) %reduce-scatter.12.cloned.1.call-update) | async-done | bytes 32784 | tf_op jit(solution)/shard_map/reduce_scatter | solution.py:75
  346.5 64.3 %all-gather.3.cloned.1.call-done = f32[2,512,512]{2,1,0:T(8,128)} async-done(((f32[2,16,512]{2,1,0:T(8,128)}), f32[2,512,512]{2,1,0:T(8,128)}) %all-gather.3.cloned.1.call-update) | async-done | bytes 2097168 | tf_op jit(solution)/shard_map/all_gather | solution.py:53
  410.8 2.0 fusion.13
  412.8 2.8 convolution_negate_fusion.1
  415.6 115.7 %reduce-scatter.14.cloned.1.call-done = f32[16,512]{1,0:T(8,128)} async-done(((f32[512,512]{1,0:T(8,128)}), f32[16,512]{1,0:T(8,128)}) %reduce-scatter.14.cloned.1.call-update) | async-done | bytes 32784 | tf_op jit(solution)/shard_map/reduce_scatter | solution.py:75
  531.3 0.0 copy-done.1
  531.3 1.4 fusion.11
  532.6 2.8 convolution_negate_fusion
  535.5 0.0 all-reduce.5.cloned.1.call-update
  535.5 0.1 copy.16
  535.6 0.7 pad_maximum_fusion
  536.3 1.2 fusion.64
  537.5 59.3 %all-gather.5.cloned.1.call-done = f32[3,512,512]{2,1,0:T(8,128)} async-done(((f32[3,16,512]{2,1,0:T(8,128)}), f32[3,512,512]{2,1,0:T(8,128)}) %all-gather.5.cloned.1.call-update) | async-done | bytes 3145744 | tf_op jit(solution)/shard_map/all_gather | solution.py:52
  596.7 3.0 fusion.63
  599.7 278.1 %all-reduce.5.cloned.1.call-done = (f32[512,512]{1,0:T(8,128)}, f32[512,512]{1,0:T(8,128)}, f32[512,512]{1,0:T(8,128)}, f32[512,512]{1,0:T(8,128)}, f32[512,512]{1,0:T(8,128)}) async-done(((f32[512,512]{1,0:T(8,128)}, f32[512,512]{1,0:T(8,128)}, f32[512,512]{1,0:T(8,128)}, f32[512,512]{1,0:T(8,128)}, f32[512,512]{1,0:T(8,128)}), (f32[512,512]{1,0:T(8,128)}, f32[512,512]{1,0:T(8,128)}, f32[512,512]{1,0:T(8,128)}, ...) | async-done | bytes 5242896 | tf_op jit(solution)/shard_map/psum | solution.py:37
  877.8 1.9 fusion.14
  879.8 0.7 fusion.25
  880.5 0.0 copy-done.7
  880.5 0.7 fusion.27
  881.2 0.7 fusion.21
  881.9 0.7 fusion.23
  882.6 0.6 fusion.3
  883.2 0.6 fusion.1
  883.8 0.6 pad_maximum_fusion.2
  884.4 1.4 fusion.9
  885.8 1.4 fusion.6
  887.2 0.6 pad_maximum_fusion.1
  (17 shorter events, 0.1 us)
Async XLA Ops:
  7.2 96.6 %copy-start = (f32[512,128]{1,0:T(8,128)S(1)}, f32[512,128]{1,0:T(8,128)}, u32[]{:S(2)}) copy-start(f32[512,128]{1,0:T(8,128)} %param.5) | copy-start | bytes 786436
  7.2 96.6 %all-reduce.7.cloned.1.call-start = ((), (), s32[]{:S(2)}) async-start(), calls=%async_computation.9 | async-start | bytes 1572864 | tf_op jit(solution)/shard_map/psum | solution.py:9
  10.3 1.1 copy-start.4
  10.3 2.0 copy-start.5
  10.3 220.8 %copy-start.3 = (f32[512,512]{1,0:T(8,128)}, f32[512,512]{1,0:T(8,128)S(1)}, u32[]{:S(2)}) copy-start(f32[512,512]{1,0:T(8,128)S(1)} %get-tuple-element.21) | copy-start | bytes 3145732
  12.3 215.1 %reduce-scatter.10.cloned.1.call-start = ((), (), s32[]{:S(2)}) async-start(), calls=%async_computation.5 | async-start | bytes 1081344
  103.8 3.5 copy-start.9
  107.2 239.2 %reduce-scatter.12.cloned.1.call-start = ((), (), s32[]{:S(2)}) async-start(), calls=%async_computation.6 | async-start | bytes 1081344 | tf_op jit(solution)/shard_map/reduce_scatter | solution.py:75
  107.3 3.0 copy-start.8
  109.7 301.1 %all-gather.3.cloned.1.call-start = ((), (), s32[]{:S(2)}) async-start(), calls=%async_computation.3 | async-start | bytes 2162688 | tf_op jit(solution)/shard_map/all_gather | solution.py:53
  110.2 421.0 %reduce-scatter.14.cloned.1.call-start = ((), (), s32[]{:S(2)}) async-start(), calls=%async_computation.7 | async-start | bytes 1081344 | tf_op jit(solution)/shard_map/reduce_scatter | solution.py:75
  112.7 484.0 %all-gather.5.cloned.1.call-start = ((), (), s32[]{:S(2)}) async-start(), calls=%async_computation.4 | async-start | bytes 3244032 | tf_op jit(solution)/shard_map/all_gather | solution.py:52
  113.3 764.5 %all-reduce.5.cloned.1.call-start = ((), (), s32[]{:S(2)}) async-start(), calls=%async_computation.8 | async-start | bytes 10485760 | tf_op jit(solution)/shard_map/psum | solution.py:37
  410.8 120.5 %copy-start.1 = (f32[2,512,512]{2,1,0:T(8,128)S(1)}, f32[2,512,512]{2,1,0:T(8,128)}, u32[]{:S(2)}) copy-start(f32[2,512,512]{2,1,0:T(8,128)} %all-gather.3.cloned.1.call-done) | copy-start | bytes 6291460
  877.8 1.9 copy-start.2
  877.8 2.6 copy-start.7
  879.7 2.1 copy-start.6
Sparse Core Ops, SparseCore 0:
  12.4 91.3 all-reduce.6
  107.3 120.0 reduce-scatter.9
  229.9 116.4 reduce-scatter.11
  348.2 62.5 all-gather.2
  413.1 118.0 reduce-scatter.13
  533.0 63.6 all-gather.4
  603.0 274.8 all-reduce.4
where the time goes:
time: 895 us
  waiting for transfers between devices  834 us (93%)
  matrix products  27.4 us (3%)
  between operations  14.3 us (2%)
  local copies, waits for them, and re-layouts  9.69 us (1%)
    psum x1, waiting for transfers between devices, total_sums(): return lax.psum(tuple(values), ('row', 'col'))  278 us
    reduce_scatter x2, waiting for transfers between devices, column_pass(): lax.psum_scatter(matmul_plain(region_inverse, right_side), 'col', scatter...  226 us
    unnamed x8, waiting for transfers between devices  115 us
    psum x1, waiting for transfers between devices, broadcast(): return lax.psum(kept, axis)  91.4 us
    all_gather x1, waiting for transfers between devices, shards(): lax.all_gather(parent_factor, 'col', axis=1, tiled=True)  64.3 us
    all_gather x1, waiting for transfers between devices, shards(): lax.all_gather(diag_inverse, 'col', axis=1, tiled=True)  59.3 us
  transfers between devices with their start and end apart: 7, of which 7 were waited for; matrix products, arithmetic and copies ran while one was open for 3% of the time, Pallas kernels for 0%

commit v1 on v0

--- a/solution.py
+++ b/solution.py
@@ -34,7 +34,7 @@
 
 
 def total_sums(values):
-    return lax.psum(tuple(values), ("row", "col"))
+    return lax.psum(lax.psum(tuple(values), "row"), "col")
 
 
 def shards(region_inverse, factor_cols, parent_factor, diag_inverse, listed):

time: 895 us -> 996 us (1.11)
  waiting for transfers between devices: 834 us -> 934 us
    psum x1 -> x2, waiting for transfers between devices: 278 us -> 370 us  [total_sums(): return lax.psum(lax.psum(tuple(values), 'row'), 'col')]
    unnamed x8 -> x9, waiting for transfers between devices: 115 us -> 116 us
  transfers between devices with their start and end apart: 7 -> 8, of which waited for: 7 -> 8; matrix products, arithmetic and copies ran while one was open for 3% -> 2% of each run, Pallas kernels for 0% -> 0%
where the time goes in v1:
time: 996 us; the launch traced here: 995 us
  waiting for transfers between devices  934 us (94%)
  matrix products  27.4 us (3%)
  between operations  14.4 us (1%)
    psum x2, waiting for transfers between devices, total_sums(): return lax.psum(lax.psum(tuple(values), 'row'), 'col')  370 us
    reduce_scatter x2, waiting for transfers between devices, column_pass(): lax.psum_scatter(matmul_plain(region_inverse, right_side), 'col', scatter...  226 us
    unnamed x9, waiting for transfers between devices  116 us
    psum x1, waiting for transfers between devices, broadcast(): return lax.psum(kept, axis)  91.4 us
    all_gather x1, waiting for transfers between devices, shards(): lax.all_gather(diag_inverse, 'col', axis=1, tiled=True)  66.6 us
    all_gather x1, waiting for transfers between devices, shards(): lax.all_gather(parent_factor, 'col', axis=1, tiled=True)  64.2 us
  transfers between devices with their start and end apart: 8, of which 8 were waited for; matrix products, arithmetic and copies ran while one was open for 2% of the time, Pallas kernels for 0%

profile of v1, /device:TPU:8, one launch (start us, length us, event | category | flops | bytes accessed | tf_op | source)
XLA Modules:
  0.0 994.8 jit_solution(2026062056038799613)
XLA Ops:
  7.2 0.0 copy-start
  7.2 0.0 all-reduce.11.cloned.1.call-start
  7.3 0.8 convert_bitcast_fusion.2
  8.1 0.1 select_reduce_fusion.1
  8.2 2.1 bitcast_multiply_fusion.1
  10.3 0.8 dynamic-slice_select_fusion.2
  11.1 0.2 copy-done.4
  11.4 0.8 dynamic-slice_select_fusion
  12.2 0.0 all-reduce.11.cloned.1.call-update
  12.2 0.0 reduce-scatter.10.cloned.1.call-start
  12.3 91.4 %all-reduce.11.cloned.1.call-done = (f32[128,512]{1,0:T(8,128)}, f32[128,512]{1,0:T(8,128)}, f32[128,512]{1,0:T(8,128)}) async-done(((f32[128,512]{1,0:T(8,128)}, f32[128,512]{1,0:T(8,128)}, f32[128,512]{1,0:T(8,128)}), (f32[128,512]{1,0:T(8,128)}, f32[128,512]{1,0:T(8,128)}, f32[128,512]{1,0:T(8,128)})) %all-reduce.11.cloned.1.call-update) | async-done | bytes 786448 | tf_op jit(solution)/shard_map/psum | solution.py:9
  103.7 0.0 copy-done
  103.7 2.0 convolution_bitcast_fusion.2
  105.7 1.4 copy.17
  107.1 0.0 reduce-scatter.10.cloned.1.call-update
  107.1 0.0 reduce-scatter.12.cloned.1.call-start
  107.2 1.0 convolution_bitcast_fusion.1
  108.2 1.3 copy.19
  109.5 0.0 reduce-scatter.12.cloned.1.call-update
  109.6 0.0 all-gather.3.cloned.1.call-start
  109.6 0.5 all-gather.3.cloned.1.call-update
  110.2 0.0 reduce-scatter.14.cloned.1.call-start
  110.2 1.0 convolution_bitcast_fusion
  111.2 1.3 copy.21
  112.6 0.0 reduce-scatter.14.cloned.1.call-update
  112.6 0.0 all-reduce.9.cloned.1.call-start
  112.7 0.1 dynamic_slice.63
  112.7 0.1 dynamic_slice.65
  112.8 0.1 dynamic_slice.67
  112.9 114.4 %reduce-scatter.10.cloned.1.call-done = f32[16,512]{1,0:T(8,128)} async-done(((f32[512,512]{1,0:T(8,128)}), f32[16,512]{1,0:T(8,128)}) %reduce-scatter.10.cloned.1.call-update) | async-done | bytes 32784
  227.3 0.9 copy.18
  228.2 2.9 convolution_negate_fusion.2
  231.1 1.9 fusion.33
  233.0 2.7 fusion.34
  235.7 110.8 %reduce-scatter.12.cloned.1.call-done = f32[16,512]{1,0:T(8,128)} async-done(((f32[512,512]{1,0:T(8,128)}), f32[16,512]{1,0:T(8,128)}) %reduce-scatter.12.cloned.1.call-update) | async-done | bytes 32784 | tf_op jit(solution)/shard_map/reduce_scatter | solution.py:75
  346.5 64.2 %all-gather.3.cloned.1.call-done = f32[2,512,512]{2,1,0:T(8,128)} async-done(((f32[2,16,512]{2,1,0:T(8,128)}), f32[2,512,512]{2,1,0:T(8,128)}) %all-gather.3.cloned.1.call-update) | async-done | bytes 2097168 | tf_op jit(solution)/shard_map/all_gather | solution.py:53
  410.7 2.0 fusion.13
  412.7 2.8 convolution_negate_fusion.1
  415.5 115.7 %reduce-scatter.14.cloned.1.call-done = f32[16,512]{1,0:T(8,128)} async-done(((f32[512,512]{1,0:T(8,128)}), f32[16,512]{1,0:T(8,128)}) %reduce-scatter.14.cloned.1.call-update) | async-done | bytes 32784 | tf_op jit(solution)/shard_map/reduce_scatter | solution.py:75
  531.2 1.4 fusion.11
  532.5 2.8 convolution_negate_fusion
  535.4 0.0 all-reduce.9.cloned.1.call-update
  535.4 0.0 all-gather.5.cloned.1.call-start
  535.5 0.7 all-gather.5.cloned.1.call-update
  536.2 0.2 all-reduce.7.cloned.1.call-start
  536.4 125.9 %all-reduce.9.cloned.1.call-done = (f32[512,512]{1,0:T(8,128)}, f32[512,512]{1,0:T(8,128)}, f32[512,512]{1,0:T(8,128)}, f32[512,512]{1,0:T(8,128)}, f32[512,512]{1,0:T(8,128)}) async-done(((f32[512,512]{1,0:T(8,128)}, f32[512,512]{1,0:T(8,128)}, f32[512,512]{1,0:T(8,128)}, f32[512,512]{1,0:T(8,128)}, f32[512,512]{1,0:T(8,128)}), (f32[512,512]{1,0:T(8,128)}, f32[512,512]{1,0:T(8,128)}, f32[512,512]{1,0:T(8,128)}, ...) | async-done | bytes 5242896 | tf_op jit(solution)/shard_map/psum | solution.py:37
  662.3 0.0 all-reduce.7.cloned.1.call-update
  662.3 0.1 copy.16
  662.4 0.7 pad_maximum_fusion
  663.1 1.1 fusion.64
  664.2 66.6 %all-gather.5.cloned.1.call-done = f32[3,512,512]{2,1,0:T(8,128)} async-done(((f32[3,16,512]{2,1,0:T(8,128)}), f32[3,512,512]{2,1,0:T(8,128)}) %all-gather.5.cloned.1.call-update) | async-done | bytes 3145744 | tf_op jit(solution)/shard_map/all_gather | solution.py:52
  730.8 3.0 fusion.63
  733.8 244.1 %all-reduce.7.cloned.1.call-done = (f32[512,512]{1,0:T(8,128)}, f32[512,512]{1,0:T(8,128)}, f32[512,512]{1,0:T(8,128)}, f32[512,512]{1,0:T(8,128)}, f32[512,512]{1,0:T(8,128)}) async-done(((f32[512,512]{1,0:T(8,128)}, f32[512,512]{1,0:T(8,128)}, f32[512,512]{1,0:T(8,128)}, f32[512,512]{1,0:T(8,128)}, f32[512,512]{1,0:T(8,128)}), (f32[512,512]{1,0:T(8,128)}, f32[512,512]{1,0:T(8,128)}, f32[512,512]{1,0:T(8,128)}, ...) | async-done | bytes 5242896 | tf_op jit(solution)/shard_map/psum | solution.py:37
  977.9 1.9 fusion.14
  979.8 0.7 fusion.25
  980.5 0.7 fusion.27
  981.2 0.7 fusion.21
  981.9 0.7 fusion.23
  982.6 0.6 fusion.3
  983.2 0.6 fusion.1
  983.8 0.6 pad_maximum_fusion.2
  984.5 1.4 fusion.9
  985.9 1.4 fusion.6
  987.3 0.6 pad_maximum_fusion.1
  (20 shorter events, 0.1 us)
Async XLA Ops:
  7.2 96.5 %copy-start = (f32[512,128]{1,0:T(8,128)S(1)}, f32[512,128]{1,0:T(8,128)}, u32[]{:S(2)}) copy-start(f32[512,128]{1,0:T(8,128)} %param.5) | copy-start | bytes 786436
  7.2 96.5 %all-reduce.11.cloned.1.call-start = ((), (), s32[]{:S(2)}) async-start(), calls=%async_computation.10 | async-start | bytes 1572864 | tf_op jit(solution)/shard_map/psum | solution.py:9
  10.3 1.1 copy-start.4
  10.3 1.9 copy-start.5
  10.3 220.8 %copy-start.3 = (f32[512,512]{1,0:T(8,128)}, f32[512,512]{1,0:T(8,128)S(1)}, u32[]{:S(2)}) copy-start(f32[512,512]{1,0:T(8,128)S(1)} %get-tuple-element.26) | copy-start | bytes 3145732
  12.2 215.1 %reduce-scatter.10.cloned.1.call-start = ((), (), s32[]{:S(2)}) async-start(), calls=%async_computation.5 | async-start | bytes 1081344
  103.7 3.5 copy-start.9
  107.1 239.3 %reduce-scatter.12.cloned.1.call-start = ((), (), s32[]{:S(2)}) async-start(), calls=%async_computation.6 | async-start | bytes 1081344 | tf_op jit(solution)/shard_map/reduce_scatter | solution.py:75
  107.2 3.0 copy-start.8
  109.6 301.1 %all-gather.3.cloned.1.call-start = ((), (), s32[]{:S(2)}) async-start(), calls=%async_computation.3 | async-start | bytes 2162688 | tf_op jit(solution)/shard_map/all_gather | solution.py:53
  110.2 421.0 %reduce-scatter.14.cloned.1.call-start = ((), (), s32[]{:S(2)}) async-start(), calls=%async_computation.7 | async-start | bytes 1081344 | tf_op jit(solution)/shard_map/reduce_scatter | solution.py:75
  112.6 549.7 %all-reduce.9.cloned.1.call-start = ((), (), s32[]{:S(2)}) async-start(), calls=%async_computation.9 | async-start | bytes 10485760 | tf_op jit(solution)/shard_map/psum | solution.py:37
  410.7 120.5 %copy-start.1 = (f32[2,512,512]{2,1,0:T(8,128)S(1)}, f32[2,512,512]{2,1,0:T(8,128)}, u32[]{:S(2)}) copy-start(f32[2,512,512]{2,1,0:T(8,128)} %all-gather.3.cloned.1.call-done) | copy-start | bytes 6291460
  535.4 195.4 %all-gather.5.cloned.1.call-start = ((), (), s32[]{:S(2)}) async-start(), calls=%async_computation.4 | async-start | bytes 3244032 | tf_op jit(solution)/shard_map/all_gather | solution.py:52
  536.2 441.7 %all-reduce.7.cloned.1.call-start = ((), (), s32[]{:S(2)}) async-start(), calls=%async_computation.8 | async-start | bytes 10485760 | tf_op jit(solution)/shard_map/psum | solution.py:37
  977.9 1.9 copy-start.2
  977.9 2.6 copy-start.7
  979.8 2.1 copy-start.6
Sparse Core Ops, SparseCore 0:
  12.3 91.3 all-reduce.10
  107.2 120.0 reduce-scatter.9
  229.8 116.5 reduce-scatter.11
  348.2 62.4 all-gather.2
  413.1 118.0 reduce-scatter.13
  535.5 126.7 all-reduce.8
  664.2 66.5 all-gather.4
  733.8 243.9 all-reduce.6
